TPU v7x, 32 devices: a whole 2x2x4 slice. The times are simulated.
32 devices in a mesh: row: 8 (over y, x, core), col: 4 (over z).
Axes of the slice: x: 2, y: 2, z: 4, core: 2. Of those that a mesh axis runs over, the one named last changes fastest.
Arguments:
- position: float32 [3, 131072], P(None, ('row', 'col')), may hold values from -6 to 6
- velocity: float32 [3, 131072], P(None, ('row', 'col')), may hold values from -4 to 4
- accel: float32 [3, 131072], P(None, ('row', 'col')), may hold values from -6 to 6
- jerk: float32 [3, 131072], P(None, ('row', 'col')), may hold values from -6 to 6
- mass: float32 [131072], P(('row', 'col')), may hold values from 3.8146973e-06 to 3.8146973e-05
- elapsed: float32 [131072], P(('row', 'col')), may hold values from 0.01 to 0.1
- active: int32 [2048], P('row'), may hold values from 0 to 131071, as said below
Outputs:
- updated: float32 [12, 2048], P(None, ('row', 'col'))
Inputs may be any that keep to these rules, and one draw needn't show every extreme that they name: `active`: distinct body indices; 0 and 131071 always appear.
All inputs are finite; a program needn't handle non-finite values.
Results may differ from a plain program's by a relative error of at most 0.0001.
Values sent between devices are 32-bit elements; how exact they have to be, the bound alone decides.
A program may use at most 64 MiB of HBM per device.

v0:
```python
import jax
import jax.numpy as jnp
from jax import lax
from jax.sharding import PartitionSpec as P

soft_sq = 0.0025


def predict(raw):
    step = raw[13][None, :]
    pos_new = (
        raw[0:3]
        + step * raw[3:6]
        + step * step / 2.0 * raw[6:9]
        + step * step * step / 6.0 * raw[9:12]
    )
    vel_new = raw[3:6] + step * raw[6:9] + step * step / 2.0 * raw[9:12]
    return (pos_new, vel_new)


def pair_terms(rows_pos, rows_vel, part):
    sep_pos = part[0:3, None, :] - rows_pos[:, :, None]
    sep_vel = part[3:6, None, :] - rows_vel[:, :, None]
    dist_sq = jnp.sum(sep_pos * sep_pos, axis=0) + soft_sq
    inv_dist = lax.rsqrt(dist_sq)
    inv_sq = inv_dist * inv_dist
    mass_term = part[6][None, :] * inv_dist * inv_sq
    radial = 3.0 * jnp.sum(sep_pos * sep_vel, axis=0) * inv_sq
    acc_part = jnp.sum(mass_term[None] * sep_pos, axis=2)
    jerk_part = jnp.sum(mass_term[None] * (sep_vel - radial[None] * sep_pos), axis=2)
    return jnp.concatenate([acc_part, jerk_part], axis=0)


def interact(rows_pos, rows_vel, cols):
    count = rows_pos.shape[1]
    width = cols.shape[1]
    block = min(width, max(128, 2**21 // count))
    while width % block:
        block = block // 2

    def advance(turn, carry):
        part = lax.dynamic_slice_in_dim(cols, turn * block, block, 1)
        return carry + pair_terms(rows_pos, rows_vel, part)

    return lax.fori_loop(0, width // block, advance, jnp.zeros((6, count), jnp.float32))


def correct(own_raw, forces):
    step = own_raw[13][None, :]
    acc_new = forces[0:3]
    jerk_new = forces[3:6]
    vel_new = (
        own_raw[3:6]
        + step / 2.0 * (own_raw[6:9] + acc_new)
        + step * step / 12.0 * (own_raw[9:12] - jerk_new)
    )
    pos_new = (
        own_raw[0:3]
        + step / 2.0 * (own_raw[3:6] + vel_new)
        + step * step / 12.0 * (own_raw[6:9] - acc_new)
    )
    return jnp.concatenate([pos_new, vel_new, acc_new, jerk_new], axis=0)


def local(position, velocity, accel, jerk, mass, elapsed, active):
    raw = jnp.concatenate(
        [position, velocity, accel, jerk, mass[None, :], elapsed[None, :]], axis=0
    )
    pos_pred, vel_pred = predict(raw)
    cols = jnp.concatenate([pos_pred, vel_pred, mass[None, :]], axis=0)
    n_col = lax.axis_size("col")
    row_at = lax.axis_index("row")
    col_at = lax.axis_index("col")
    body_dev = raw.shape[1]
    act_row = active.shape[0]
    linear = row_at * n_col + col_at
    base = linear * body_dev
    every_index = lax.all_gather(active, "row", axis=0, tiled=True)
    offset = every_index - base
    inside = (offset >= 0) & (offset < body_dev)
    taken = jnp.take(raw, jnp.clip(offset, 0, body_dev - 1), axis=1)
    picked = jnp.where(inside[None, :], taken, jnp.zeros_like(taken))
    mine = lax.psum_scatter(picked, "row", scatter_dimension=1, tiled=True)
    rows_raw = lax.psum(mine, "col")
    rows_pos, rows_vel = predict(rows_raw)
    partial_value = interact(rows_pos, rows_vel, lax.all_gather(cols, "row", axis=1, tiled=True))
    forces = lax.psum_scatter(partial_value, "col", scatter_dimension=1, tiled=True)
    share = act_row // n_col
    own_raw = lax.dynamic_slice_in_dim(rows_raw, col_at * share, share, 1)
    return correct(own_raw, forces)


def solution(mesh):
    return jax.shard_map(
        local,
        mesh=mesh,
        in_specs=(
            P(None, ("row", "col")),
            P(None, ("row", "col")),
            P(None, ("row", "col")),
            P(None, ("row", "col")),
            P(("row", "col")),
            P(("row", "col")),
            P("row"),
        ),
        out_specs=P(None, ("row", "col")),
        check_vma=False,
    )
```

profile of v0, /device:TPU:1, one launch (start us, length us, event | category | flops | bytes accessed | tf_op | source)
XLA Modules:
  0.0 251.3 jit_solution(1446033047032847611)
XLA Ops:
  6.5 0.0 reduce-scatter.5.cloned.1.call-start
  6.5 10.4 %all-gather = s32[8,1,256]{2,1,0:T(1,128)S(1)} all-gather(s32[1,1,256]{2,1,0:T(1,128)} %bitcast.29), channel_id=1, replica_groups=mesh['row'=8,'col'=4] {'row'}, dimensions={0}, use_global_device_ids=true | all-gather | bytes 9216 | tf_op jit(solution)/shard_map/all_gather | solution.py:78
  17.0 2.9 %concatenate.17 = f32[14,4096]{1,0:T(8,128)S(1)} concatenate(f32[3,4096]{1,0:T(4,128)} %param.9, f32[3,4096]{1,0:T(4,128)} %param.10, f32[3,4096]{1,0:T(4,128)} %param.11, f32[3,4096]{1,0:T(4,128)} %param.12, f32[1,4096]{1,0:T(1,128)} %bitcast.23, f32[1,4096]{1,0:T(1,128)} %bitcast.20), dimensions={0} | concatenate | bytes 458752 | tf_op jit(solution)/shard_map/concatenate | solution.py:66
  19.9 0.6 copy.67
  20.5 5.5 %gather_fusion = f32[2048,14]{1,0:T(8,128)S(1)} fusion(f32[14,4096]{0,1:T(8,128)S(1)} %copy.67, s32[2048]{0:T(1024)S(1)} %fusion.6), kind=kCustom, calls=%fused_computation | custom fusion | bytes 237568 | tf_op jit(solution)/shard_map/jit(_take)/gather | solution.py:81
  26.0 0.3 copy.68
  26.4 0.7 select_bitcast_fusion
  27.0 0.0 reduce-scatter.5.cloned.1.call-update
  27.1 0.0 reduce-scatter.7.cloned.1.call-start
  27.1 0.7 fusion.5
  27.8 1.0 multiply_add_fusion.1
  28.8 0.8 pad_maximum_fusion
  29.6 11.1 %all_gather.7 = f32[7,32768]{1,0:T(8,128)S(1)} all-gather(f32[7,4096]{1,0:T(8,128)S(1)} %pad_maximum_fusion), channel_id=1, replica_groups=mesh['row'=8,'col'=4] {'row'}, dimensions={1}, use_global_device_ids=true | all-gather | bytes 1032192 | tf_op jit(solution)/shard_map/all_gather | solution.py:86
  40.7 19.2 %reduce-scatter.5.cloned.1.call-done = f32[14,256]{1,0:T(8,128)} async-done(((f32[14,2048]{1,0:T(8,128)}), f32[14,256]{1,0:T(8,128)}) %reduce-scatter.5.cloned.1.call-update) | async-done | bytes 14352 | tf_op jit(solution)/shard_map/reduce_scatter | solution.py:83
  59.9 15.6 %psum.7 = f32[14,256]{1,0:T(8,128)S(1)} all-reduce(f32[14,256]{1,0:T(8,128)} %reduce-scatter.5.cloned.1.call-done), channel_id=1, replica_groups=mesh['row'=8,'col'=4] {'col'}, use_global_device_ids=true, to_apply=%region_1.2 | all-reduce | flops 3584 | bytes 28672 | tf_op jit(solution)/shard_map/psum | solution.py:84
  75.5 147.8 %while.14 = (s32[]{:T(128)}, f32[6,256]{1,0:T(8,128)S(1)}, f32[7,32768]{1,0:T(8,128)S(1)}, f32[3,256]{1,0:T(4,128)S(1)}, f32[3,256]{1,0:T(4,128)S(1)}, /*index=5...) while((s32[]{:T(128)}, f32[6,256]{1,0:T(8,128)S(1)}, ...), condition=%wide.region_7.8_spmd.clone, body=%wide.region_2.0_spmd.clone.sunk | while | flops 96472072 | bytes 68030664 | solution.py:45
  75.5 0.1 fusion.19
  75.7 17.3 %fusion.20 = (f32[256,8192]{1,0:T(8,128)}, f32[256,8192]{1,0:T(8,128)}) fusion(f32[3,256]{1,0:T(4,128)S(1)} %get-tuple-element.221, f32[3,8192]{1,0:T(4,128)S(1)} %get-tuple-element.188, f32[3,256]{1,0:T(4,128)S(1)} %get-tuple-element.222, f32[3,8192]{1,0:T(4,128)S(1)} %get-tuple-element.189), kind=kLoop, calls=%fused_computation.8.clone.1 | loop fusion | flops 33554432 | bytes 16979968 | tf_op jit(solution)/shard_map/while/body/eval_jaxpr/reduce_sum | solution.py:24
  92.9 0.1 dynamic-slice.30
  93.1 7.2 %multiply_multiply_fusion.7 = (f32[256,8192]{1,0:T(8,128)S(1)}, f32[256,8192]{1,0:T(8,128)S(1)}) fusion(f32[256,8192]{1,0:T(8,128)} %get-tuple-element.190, f32[256,8192]{1,0:T(8,128)} %get-tuple-element.191, f32[8192]{0:T(1024)S(1)} %bitcast.18), kind=kLoop, calls=%fused_computation.11.clone.1 | loop fusion | flops 12582912 | bytes 33587200 | tf_op jit(solution)/shard_map/while/body/eval_jaxpr/mul | solution.py:28
  100.2 12.2 %fusion.21 = (f32[3,256]{1,0:T(4,128)S(1)}, f32[3,256]{1,0:T(4,128)S(1)}) fusion(f32[256,8192]{1,0:T(8,128)S(1)} %get-tuple-element.192, f32[3,256]{1,0:T(4,128)S(1)} %get-tuple-element.221, f32[3,8192]{1,0:T(4,128)S(1)} %get-tuple-element.188, f32[256,8192]{1,0:T(8,128)S(1)} %get-tuple-element.193, f32[3,256]{1,0:T(4,128)S(1)} %get-tuple-element.222, ...), kind=kLoop, calls=%fused_computation.9.clone.1 | loop fusion | flops 50330112 | bytes 16986112 | tf_op jit(solution)/shard_map/while/body/eval_jaxpr/reduce_sum | solution.py:29
  112.5 0.1 fusion.19
  112.6 17.3 %fusion.20 = (f32[256,8192]{1,0:T(8,128)}, f32[256,8192]{1,0:T(8,128)}) fusion(f32[3,256]{1,0:T(4,128)S(1)} %get-tuple-element.221, f32[3,8192]{1,0:T(4,128)S(1)} %get-tuple-element.188, f32[3,256]{1,0:T(4,128)S(1)} %get-tuple-element.222, f32[3,8192]{1,0:T(4,128)S(1)} %get-tuple-element.189), kind=kLoop, calls=%fused_computation.8.clone.1 | loop fusion | flops 33554432 | bytes 16979968 | tf_op jit(solution)/shard_map/while/body/eval_jaxpr/reduce_sum | solution.py:24
  129.9 0.1 dynamic-slice.30
  130.0 7.2 %multiply_multiply_fusion.7 = (f32[256,8192]{1,0:T(8,128)S(1)}, f32[256,8192]{1,0:T(8,128)S(1)}) fusion(f32[256,8192]{1,0:T(8,128)} %get-tuple-element.190, f32[256,8192]{1,0:T(8,128)} %get-tuple-element.191, f32[8192]{0:T(1024)S(1)} %bitcast.18), kind=kLoop, calls=%fused_computation.11.clone.1 | loop fusion | flops 12582912 | bytes 33587200 | tf_op jit(solution)/shard_map/while/body/eval_jaxpr/mul | solution.py:28
  137.2 12.2 %fusion.21 = (f32[3,256]{1,0:T(4,128)S(1)}, f32[3,256]{1,0:T(4,128)S(1)}) fusion(f32[256,8192]{1,0:T(8,128)S(1)} %get-tuple-element.192, f32[3,256]{1,0:T(4,128)S(1)} %get-tuple-element.221, f32[3,8192]{1,0:T(4,128)S(1)} %get-tuple-element.188, f32[256,8192]{1,0:T(8,128)S(1)} %get-tuple-element.193, f32[3,256]{1,0:T(4,128)S(1)} %get-tuple-element.222, ...), kind=kLoop, calls=%fused_computation.9.clone.1 | loop fusion | flops 50330112 | bytes 16986112 | tf_op jit(solution)/shard_map/while/body/eval_jaxpr/reduce_sum | solution.py:29
  149.4 0.1 fusion.19
  149.5 17.3 %fusion.20 = (f32[256,8192]{1,0:T(8,128)}, f32[256,8192]{1,0:T(8,128)}) fusion(f32[3,256]{1,0:T(4,128)S(1)} %get-tuple-element.221, f32[3,8192]{1,0:T(4,128)S(1)} %get-tuple-element.188, f32[3,256]{1,0:T(4,128)S(1)} %get-tuple-element.222, f32[3,8192]{1,0:T(4,128)S(1)} %get-tuple-element.189), kind=kLoop, calls=%fused_computation.8.clone.1 | loop fusion | flops 33554432 | bytes 16979968 | tf_op jit(solution)/shard_map/while/body/eval_jaxpr/reduce_sum | solution.py:24
  166.8 0.1 dynamic-slice.30
  167.0 7.2 %multiply_multiply_fusion.7 = (f32[256,8192]{1,0:T(8,128)S(1)}, f32[256,8192]{1,0:T(8,128)S(1)}) fusion(f32[256,8192]{1,0:T(8,128)} %get-tuple-element.190, f32[256,8192]{1,0:T(8,128)} %get-tuple-element.191, f32[8192]{0:T(1024)S(1)} %bitcast.18), kind=kLoop, calls=%fused_computation.11.clone.1 | loop fusion | flops 12582912 | bytes 33587200 | tf_op jit(solution)/shard_map/while/body/eval_jaxpr/mul | solution.py:28
  174.1 12.2 %fusion.21 = (f32[3,256]{1,0:T(4,128)S(1)}, f32[3,256]{1,0:T(4,128)S(1)}) fusion(f32[256,8192]{1,0:T(8,128)S(1)} %get-tuple-element.192, f32[3,256]{1,0:T(4,128)S(1)} %get-tuple-element.221, f32[3,8192]{1,0:T(4,128)S(1)} %get-tuple-element.188, f32[256,8192]{1,0:T(8,128)S(1)} %get-tuple-element.193, f32[3,256]{1,0:T(4,128)S(1)} %get-tuple-element.222, ...), kind=kLoop, calls=%fused_computation.9.clone.1 | loop fusion | flops 50330112 | bytes 16986112 | tf_op jit(solution)/shard_map/while/body/eval_jaxpr/reduce_sum | solution.py:29
  186.3 0.1 fusion.19
  186.5 17.3 %fusion.20 = (f32[256,8192]{1,0:T(8,128)}, f32[256,8192]{1,0:T(8,128)}) fusion(f32[3,256]{1,0:T(4,128)S(1)} %get-tuple-element.221, f32[3,8192]{1,0:T(4,128)S(1)} %get-tuple-element.188, f32[3,256]{1,0:T(4,128)S(1)} %get-tuple-element.222, f32[3,8192]{1,0:T(4,128)S(1)} %get-tuple-element.189), kind=kLoop, calls=%fused_computation.8.clone.1 | loop fusion | flops 33554432 | bytes 16979968 | tf_op jit(solution)/shard_map/while/body/eval_jaxpr/reduce_sum | solution.py:24
  203.8 0.1 dynamic-slice.30
  203.9 7.2 %multiply_multiply_fusion.7 = (f32[256,8192]{1,0:T(8,128)S(1)}, f32[256,8192]{1,0:T(8,128)S(1)}) fusion(f32[256,8192]{1,0:T(8,128)} %get-tuple-element.190, f32[256,8192]{1,0:T(8,128)} %get-tuple-element.191, f32[8192]{0:T(1024)S(1)} %bitcast.18), kind=kLoop, calls=%fused_computation.11.clone.1 | loop fusion | flops 12582912 | bytes 33587200 | tf_op jit(solution)/shard_map/while/body/eval_jaxpr/mul | solution.py:28
  211.1 12.2 %fusion.21 = (f32[3,256]{1,0:T(4,128)S(1)}, f32[3,256]{1,0:T(4,128)S(1)}) fusion(f32[256,8192]{1,0:T(8,128)S(1)} %get-tuple-element.192, f32[3,256]{1,0:T(4,128)S(1)} %get-tuple-element.221, f32[3,8192]{1,0:T(4,128)S(1)} %get-tuple-element.188, f32[256,8192]{1,0:T(8,128)S(1)} %get-tuple-element.193, f32[3,256]{1,0:T(4,128)S(1)} %get-tuple-element.222, ...), kind=kLoop, calls=%fused_computation.9.clone.1 | loop fusion | flops 50330112 | bytes 16986112 | tf_op jit(solution)/shard_map/while/body/eval_jaxpr/reduce_sum | solution.py:29
  223.3 0.8 copy.69
  224.1 0.0 reduce-scatter.7.cloned.1.call-update
  224.1 0.1 multiply_bitcast_fusion.1
  224.2 18.7 %reduce-scatter.7.cloned.1.call-done = f32[64,6]{1,0:T(8,128)} async-done(((f32[256,6]{1,0:T(8,128)}), f32[64,6]{1,0:T(8,128)}) %reduce-scatter.7.cloned.1.call-update) | async-done | bytes 1552
  242.9 0.8 copy.70
  243.7 0.1 fusion.11
  243.8 0.6 pad_maximum_fusion.1
  (12 shorter events, 0.1 us)
Async XLA Ops:
  6.5 53.3 %reduce-scatter.5.cloned.1.call-start = ((), (), s32[]{:S(2)}) async-start(), calls=%async_computation.2 | async-start | bytes 147456 | tf_op jit(solution)/shard_map/reduce_scatter | solution.py:83
  27.1 215.8 %reduce-scatter.7.cloned.1.call-start = ((), (), s32[]{:S(2)}) async-start(), calls=%async_computation.3 | async-start | bytes 163840
Sparse Core Ops, SparseCore 0:
  27.2 32.6 reduce-scatter.4
  224.2 18.6 reduce-scatter.6
where the time goes:
time: 255 us; the launch traced here: 251 us
  other arithmetic  150 us (59%)
  waiting for transfers between devices  38 us (15%)
  blocking collectives  37 us (15%)
  between operations  13.5 us (5%)
  local copies, waits for them, and re-layouts  12 us (5%)
    reduce_sum x4, other arithmetic, pair_terms(): dist_sq = jnp.sum(sep_pos * sep_pos, axis=0) + soft_sq  69.1 us
    reduce_sum x4, other arithmetic, pair_terms(): acc_part = jnp.sum(mass_term[None] * sep_pos, axis=2)  48.7 us
    mul x4, other arithmetic, pair_terms(): radial = 3.0 * jnp.sum(sep_pos * sep_vel, axis=0) * inv_sq  28.7 us
    reduce_scatter x1, waiting for transfers between devices, local(): mine = lax.psum_scatter(picked, 'row', scatter_dimension=1, tiled=True)  19.2 us
    unnamed x3, waiting for transfers between devices  18.7 us
    psum x1, blocking collectives, local(): rows_raw = lax.psum(mine, 'col')  15.6 us
    all_gather x1, blocking collectives, local(): lax.all_gather(cols, 'row', axis=1, tiled=True)  11.1 us
    all_gather x1, blocking collectives, local(): every_index = lax.all_gather(active, 'row', axis=0, tiled=True)  10.4 us
  transfers between devices with their start and end apart: 2, of which 2 were waited for; matrix products, arithmetic and copies ran while one was open for 1% of the time, Pallas kernels for 0%

commit v1 on v0

v1 whole, which is shorter than its diff:
```python
import functools

import jax
import jax.numpy as jnp
from jax import lax
from jax.experimental import pallas as pl
from jax.experimental.pallas import tpu as pltpu
from jax.sharding import PartitionSpec as P

soft_sq = 0.0025
f32 = jnp.float32
bf16 = jnp.bfloat16
MESH = pl.DeviceIdType.MESH
WIDE = 128

LEFT = (0, 0, 1, 1, 0, 2)
RIGHT = (0, 1, 0, 1, 2, 0)


def split3(x):
    high = x.astype(bf16).astype(f32)
    rest = x - high
    mid = rest.astype(bf16).astype(f32)
    return high, mid, rest - mid


def take(pieces, order):
    return [pieces[t] for t in order]


def predict(pos, vel, acc, jerk, step):
    pos_new = pos + step * vel + step * step / 2.0 * acc + step * step * step / 6.0 * jerk
    vel_new = vel + step * acc + step * step / 2.0 * jerk
    return pos_new, vel_new


def source_rows(p, q):
    sp, sq = split3(p), split3(q)
    n = split3(jnp.sum(p * p, axis=0, keepdims=True))
    d = split3(jnp.sum(p * q, axis=0, keepdims=True))
    one = jnp.ones_like(n[0])
    return jnp.concatenate(
        take(sp, LEFT) + take(sq, LEFT) + list(n) + list(d) + [one, one, one]
        + [jnp.zeros((WIDE - 45, p.shape[1]), f32)],
        axis=0,
    )


def active_rows(p, q):
    width = p.shape[1]
    sp, sq = split3(p), split3(q)
    n = split3(jnp.sum(p * p, axis=0, keepdims=True) + soft_sq)
    d = split3(jnp.sum(p * q, axis=0, keepdims=True))
    one = jnp.ones_like(n[0])
    z18, z3 = jnp.zeros((18, width), f32), jnp.zeros((3, width), f32)
    tail = jnp.zeros((WIDE - 45, width), f32)
    for_sq = jnp.concatenate(
        [-2.0 * t for t in take(sp, RIGHT)] + [z18, one, one, one, z3] + list(n) + [tail], axis=0
    )
    for_rw = jnp.concatenate(
        [-t for t in take(sq, RIGHT)] + [-t for t in take(sp, RIGHT)] + [z3, one, one, one] + list(d) + [tail],
        axis=0,
    )
    return for_sq.astype(bf16), for_rw.astype(bf16)


def weight_rows(p, q, m):
    return jnp.concatenate(
        list(split3(m * p)) + list(split3(m * q)) + list(split3(m)) + [jnp.zeros((32 - 21, p.shape[1]), f32)],
        axis=0,
    )


def three(a, k):
    return a[k : k + 3] + a[k + 3 : k + 6] + a[k + 6 : k + 9]


def padded(x, rows, lanes):
    if x.shape[0] < rows:
        x = jnp.concatenate([x, jnp.zeros((rows - x.shape[0], x.shape[1]), f32)], axis=0)
    if x.shape[1] < lanes:
        x = jnp.concatenate([x, jnp.zeros((rows, lanes - x.shape[1]), f32)], axis=1)
    return x


def kernel(
    n_row, n_col, share, pos_ref, vel_ref, acc_ref, jerk_ref, mass_ref, step_ref, act_ref, out_ref,
    idx, table, left, weight, mid_ref, give, got, state, f_give, f_got,
    idx_s, idx_r, give_s, give_r, st_s, st_r, f_s, f_r,
):
    n_dev = n_row * n_col
    bodies = pos_ref.shape[1]
    chunks = bodies // WIDE
    act_row = share * n_col
    row, col = lax.axis_index("row"), lax.axis_index("col")
    me = row * n_col + col
    base = me * bodies

    def other(k):
        return lax.rem(me + k, n_dev)

    def at(d):
        return (lax.div(d, n_col), lax.rem(d, n_col))

    def send(src, dst, ss, rs, dev):
        return pltpu.make_async_remote_copy(
            src_ref=src, dst_ref=dst, send_sem=ss, recv_sem=rs, device_id=dev, device_id_type=MESH
        )

    barrier = pltpu.get_barrier_semaphore()

    def greet(k, _):
        pl.semaphore_signal(barrier, inc=1, device_id=at(other(k)), device_id_type=MESH)
        return 0

    lax.fori_loop(1, n_dev, greet, 0)

    for c in range(chunks):
        lane = pl.ds(c * WIDE, WIDE)
        raw = jnp.concatenate(
            [pos_ref[:, lane], vel_ref[:, lane], acc_ref[:, lane], jerk_ref[:, lane], step_ref[:, lane],
             jnp.zeros((3, WIDE), f32)], axis=0,
        )
        for t, piece in enumerate(split3(raw)):
            table[t, pl.ds(c * 16, 16), :] = piece.astype(bf16)

    pl.semaphore_wait(barrier, n_dev - 1)

    def idx_copy(r, slot):
        return send(act_ref, idx.at[slot], idx_s.at[r], idx_r.at[slot], (r, col))

    def idx_start(k, _):
        idx_copy(lax.rem(row + k, n_row), row).start()
        return 0

    lax.fori_loop(1, n_row, idx_start, 0)
    idx[row] = act_ref[...]

    def give_copy(d, slot):
        return send(give.at[d], got.at[slot], give_s.at[d], give_r.at[slot], at(d))

    def pick(k, _):
        r = lax.rem(row + k, n_row)

        @pl.when(k > 0)
        def _():
            idx_copy(r, r).wait_recv()

        offset = idx[r] - base
        high = lax.shift_right_arithmetic(offset, 7)
        low = lax.bitwise_and(offset, 127)
        hot = jnp.where(lax.broadcasted_iota(jnp.int32, (WIDE, act_row), 0) == low, 1.0, 0.0).astype(bf16)
        found = jnp.dot(table[0], hot, preferred_element_type=f32)
        found = found + jnp.dot(table[1], hot, preferred_element_type=f32)
        found = found + jnp.dot(table[2], hot, preferred_element_type=f32)
        mine = jnp.zeros((16, act_row), f32)
        for c in range(chunks):
            mine = mine + jnp.where(high == c, found[c * 16 : (c + 1) * 16], 0.0)
        for c in range(n_col):
            part = mine[:, c * share : (c + 1) * share]
            d = r * n_col + c
            give[d] = padded(jnp.concatenate([part[0:8], part[8:16]], axis=1), 8, WIDE)
        for c in range(n_col):
            d = r * n_col + c

            @pl.when(d != me)
            def _():
                give_copy(d, me).start()

        return 0

    lax.fori_loop(0, n_row, pick, 0)

    p_all, q_all = predict(pos_ref[...], vel_ref[...], acc_ref[...], jerk_ref[...], step_ref[...])
    p_mid = jnp.mean(p_all, axis=1, keepdims=True)
    q_mid = jnp.mean(q_all, axis=1, keepdims=True)
    mid_ref[0:3, :] = jnp.broadcast_to(p_mid, (3, WIDE))
    mid_ref[3:6, :] = jnp.broadcast_to(q_mid, (3, WIDE))
    piece = min(512, bodies)
    for t in range(0, bodies, piece):
        lane = pl.ds(t, piece)
        p, q = predict(pos_ref[:, lane], vel_ref[:, lane], acc_ref[:, lane], jerk_ref[:, lane], step_ref[:, lane])
        p, q = p - p_mid, q - q_mid
        left[lane, :] = source_rows(p, q).T.astype(bf16)
        weight[:, lane] = weight_rows(p, q, mass_ref[:, lane]).astype(bf16)

    def gather(k, total):
        d = other(k)
        give_copy(d, d).wait_recv()
        return total + got[d]

    slab = lax.fori_loop(1, n_dev, gather, give[me])
    x0, v0, a0 = slab[0:3, 0:share], slab[3:6, 0:share], jnp.concatenate(
        [slab[6:8, 0:share], slab[0:1, share : 2 * share]], axis=0)
    j0, step = slab[1:4, share : 2 * share], slab[4:5, share : 2 * share]
    p_own, q_own = predict(x0, v0, a0, j0, step)
    state[me] = padded(jnp.concatenate([p_own, q_own], axis=1), 4, WIDE)

    def state_copy(d, slot):
        return send(state.at[me], state.at[slot], st_s.at[d], st_r.at[slot], at(d))

    def state_start(k, _):
        state_copy(other(k), me).start()
        return 0

    lax.fori_loop(1, n_dev, state_start, 0)

    def f_copy(d, slot):
        return send(f_give.at[d], f_got.at[slot], f_s.at[d], f_r.at[slot], at(d))

    def meet(k, _):
        r = lax.rem(row + k, n_row)
        for c in range(n_col):
            d = r * n_col + c

            @pl.when(d != me)
            def _():
                state_copy(d, d).wait_recv()

        slabs = [state[r * n_col + c] for c in range(n_col)]
        p = jnp.concatenate([s[0:3, 0:share] for s in slabs], axis=1) - mid_ref[0:3, 0:1]
        q = jnp.concatenate([s[0:3, share : 2 * share] for s in slabs], axis=1) - mid_ref[3:6, 0:1]
        for_sq, for_rw = active_rows(p, q)
        b = left[...]
        qt = weight[...]
        dist_sq = jnp.dot(b, for_sq, preferred_element_type=f32)
        r_dot_w = jnp.dot(b, for_rw, preferred_element_type=f32)
        inv = lax.rsqrt(dist_sq)
        inv_sq = inv * inv
        w = inv_sq * inv
        v = (w * inv_sq) * r_dot_w
        wh, vh = w.astype(bf16), v.astype(bf16)
        wl = (w - wh.astype(f32)).astype(bf16)
        vl = (v - vh.astype(f32)).astype(bf16)
        ws = jnp.dot(qt, wh, preferred_element_type=f32) + jnp.dot(qt, wl, preferred_element_type=f32)
        vs = jnp.dot(qt, vh, preferred_element_type=f32) + jnp.dot(qt, vl, preferred_element_type=f32)
        w_sum = ws[18:19] + ws[19:20] + ws[20:21]
        v_sum = vs[18:19] + vs[19:20] + vs[20:21]
        acc = three(ws, 0) - p * w_sum
        jerk = (three(ws, 9) - q * w_sum) - 3.0 * (three(vs, 0) - p * v_sum)
        for c in range(n_col):
            lane = slice(c * share, (c + 1) * share)
            f_give[r * n_col + c] = padded(jnp.concatenate([acc[:, lane], jerk[:, lane]], axis=1), 4, WIDE)
        for c in range(n_col):
            d = r * n_col + c

            @pl.when(d != me)
            def _():
                f_copy(d, me).start()

        return 0

    lax.fori_loop(0, n_row, meet, 0)

    def add_up(k, total):
        d = other(k)
        f_copy(d, d).wait_recv()
        return total + f_got[d]

    forces = lax.fori_loop(1, n_dev, add_up, f_give[me])
    a1, j1 = forces[0:3, 0:share], forces[0:3, share : 2 * share]
    v1 = v0 + step / 2.0 * (a0 + a1) + step * step / 12.0 * (j0 - j1)
    x1 = x0 + step / 2.0 * (v0 + v1) + step * step / 12.0 * (a0 - a1)
    out_ref[...] = jnp.concatenate([x1, v1, a1, j1], axis=0)

    def idx_end(k, _):
        idx_copy(lax.rem(row + k, n_row), row).wait_send()
        return 0

    lax.fori_loop(1, n_row, idx_end, 0)

    def all_end(k, _):
        d = other(k)
        give_copy(d, me).wait_send()
        state_copy(d, me).wait_send()
        f_copy(d, me).wait_send()
        return 0

    lax.fori_loop(1, n_dev, all_end, 0)


def solution(mesh):
    n_row, n_col = mesh.shape["row"], mesh.shape["col"]
    n_dev = n_row * n_col

    def local(position, velocity, accel, jerk, mass, elapsed, active):
        bodies = position.shape[1]
        act_row = active.shape[0]
        share = act_row // n_col
        dma = pltpu.SemaphoreType.DMA
        return pl.pallas_call(
            functools.partial(kernel, n_row, n_col, share),
            out_shape=jax.ShapeDtypeStruct((12, share), f32),
            in_specs=[pl.BlockSpec(memory_space=pltpu.VMEM)] * 7,
            out_specs=pl.BlockSpec(memory_space=pltpu.VMEM),
            scratch_shapes=[
                pltpu.VMEM((n_row, 1, act_row), jnp.int32),
                pltpu.VMEM((3, bodies // WIDE * 16, WIDE), bf16),
                pltpu.VMEM((bodies, WIDE), bf16),
                pltpu.VMEM((32, bodies), bf16),
                pltpu.VMEM((8, WIDE), f32),
                pltpu.VMEM((n_dev, 8, WIDE), f32),
                pltpu.VMEM((n_dev, 8, WIDE), f32),
                pltpu.VMEM((n_dev, 4, WIDE), f32),
                pltpu.VMEM((n_dev, 4, WIDE), f32),
                pltpu.VMEM((n_dev, 4, WIDE), f32),
                dma((n_row,)), dma((n_row,)),
                dma((n_dev,)), dma((n_dev,)),
                dma((n_dev,)), dma((n_dev,)),
                dma((n_dev,)), dma((n_dev,)),
            ],
            compiler_params=pltpu.CompilerParams(
                collective_id=0, has_side_effects=True, vmem_limit_bytes=48 * 2**20
            ),
        )(position, velocity, accel, jerk, mass[None, :], elapsed[None, :], active[None, :])

    both = P(None, ("row", "col"))
    one = P(("row", "col"))
    return jax.shard_map(
        local, mesh=mesh, in_specs=(both, both, both, both, one, one, P("row")), out_specs=both, check_vma=False
    )
```

time: 255 us -> 54.6 us (0.21); the launches traced: 251 us -> 54.2 us
  other arithmetic: 150 us -> 0 us
  Pallas kernels: 0 us -> 48.1 us
  waiting for transfers between devices: 38 us -> 0 us
  blocking collectives: 37 us -> 0 us
  between operations: 13.5 us -> 0.02 us
  local copies, waits for them, and re-layouts: 12 us -> 6.07 us
    reduce_sum x8 -> x0, other arithmetic: 118 us -> none  [the longest x4 69.1 us: pair_terms(): dist_sq = jnp.sum(sep_pos * sep_pos, axis=0) + soft_sq]
    pallas_call x0 -> x1, Pallas kernels: none -> 48.1 us  [local(): pl.pallas_call(functools.partial(kernel, n_row, n_col, share), out_shape=...]
    mul x5 -> x0, other arithmetic: 28.7 us -> none  [the longest x4 28.7 us: pair_terms(): radial = 3.0 * jnp.sum(sep_pos * sep_vel, axis=0) * inv_sq]
    all_gather x2 -> x0, blocking collectives: 21.5 us -> none  [the longest x1 11.1 us: local(): lax.all_gather(cols, 'row', axis=1, tiled=True)]
    reduce_scatter x1 -> x0, waiting for transfers between devices: 19.2 us -> none  [local(): mine = lax.psum_scatter(picked, 'row', scatter_dimension=1, tiled=True)]
    unnamed x3 -> x0, waiting for transfers between devices: 18.7 us -> none
    psum x1 -> x0, blocking collectives: 15.6 us -> none  [local(): rows_raw = lax.psum(mine, 'col')]
    gather x2 -> x0, local copies, waits for them, and re-layouts: 5.8 us -> none  [local(): taken = jnp.take(raw, jnp.clip(offset, 0, body_dev - 1), axis=1)]
  transfers between devices with their start and end apart: 2 -> 0, of which waited for: 2 -> 0; matrix products, arithmetic and copies ran while one was open for 1% -> 0% of each run, Pallas kernels for 0% -> 0%
where the time goes in v1:
time: 54.6 us; the launch traced here: 54.2 us
  Pallas kernels  48.1 us (88%)
  local copies, waits for them, and re-layouts  6.07 us (11%)
    pallas_call x1, Pallas kernels, local(): pl.pallas_call(functools.partial(kernel, n_row, n_col, share), out_shape=...  48.1 us
    unnamed x15, local copies, waits for them, and re-layouts  6.07 us

profile of v1, /device:TPU:1, one launch (start us, length us, event | category | flops | bytes accessed | tf_op | source)
XLA Modules:
  0.0 54.2 jit_solution(10705466350425317981)
XLA Ops:
  0.0 0.0 copy-start.6
  0.0 0.7 %copy-done.6 = s32[256]{0:T(256)S(1)} copy-done((s32[256]{0:T(256)S(1)}, s32[256]{0:T(256)}, u32[]{:S(2)}) %copy-start.6) | copy-done | bytes 1048
  0.7 0.0 copy-start
  0.7 0.8 %copy-done = f32[3,4096]{1,0:T(4,128)S(1)} copy-done((f32[3,4096]{1,0:T(4,128)S(1)}, f32[3,4096]{1,0:T(4,128)}, u32[]{:S(2)}) %copy-start) | copy-done | bytes 49176
  1.5 0.0 copy-start.1
  1.5 0.8 %copy-done.1 = f32[3,4096]{1,0:T(4,128)S(1)} copy-done((f32[3,4096]{1,0:T(4,128)S(1)}, f32[3,4096]{1,0:T(4,128)}, u32[]{:S(2)}) %copy-start.1) | copy-done | bytes 49176
  2.4 0.0 copy-start.2
  2.4 0.8 %copy-done.2 = f32[3,4096]{1,0:T(4,128)S(1)} copy-done((f32[3,4096]{1,0:T(4,128)S(1)}, f32[3,4096]{1,0:T(4,128)}, u32[]{:S(2)}) %copy-start.2) | copy-done | bytes 49176
  3.2 0.0 copy-start.3
  3.2 0.8 %copy-done.3 = f32[3,4096]{1,0:T(4,128)S(1)} copy-done((f32[3,4096]{1,0:T(4,128)S(1)}, f32[3,4096]{1,0:T(4,128)}, u32[]{:S(2)}) %copy-start.3) | copy-done | bytes 49176
  4.0 0.0 copy-start.4
  4.0 0.7 %copy-done.4 = f32[4096]{0:T(1024)S(1)} copy-done((f32[4096]{0:T(1024)S(1)}, f32[4096]{0:T(1024)}, u32[]{:S(2)}) %copy-start.4) | copy-done | bytes 16408
  4.8 0.0 copy-start.5
  4.8 0.7 %copy-done.5 = f32[4096]{0:T(1024)S(1)} copy-done((f32[4096]{0:T(1024)S(1)}, f32[4096]{0:T(1024)}, u32[]{:S(2)}) %copy-start.5) | copy-done | bytes 16408
  5.5 48.1 %shard_map.73 = f32[12,64]{1,0:T(8,128)S(1)} custom-call(f32[3,4096]{1,0:T(4,128)S(1)} %copy-done, f32[3,4096]{1,0:T(4,128)S(1)} %copy-done.1, f32[3,4096]{1,0:T(4,128)S(1)} %copy-done.2, f32[3,4096]{1,0:T(4,128)S(1)} %copy-done.3, f32[1,4096]{1,0:T(1,128)S(1)} %bitcast.3, f32[1,4096]{1,0:T(1,128)S(1)} %bitcast.4, s32[1,256]{1,0:T(1,128)S(1)} %bitcast.5), custom_call_target="tpu_custom_call" | custom-call | tf_op jit(solution)/shard_map/pallas_call | solution.py:291
  53.6 0.6 %copy.9 = f32[12,64]{1,0:T(8,128)} copy(f32[12,64]{1,0:T(8,128)S(1)} %shard_map.73) | data formatting | bytes 6144
Async XLA Ops:
  0.0 0.7 %copy-start.6 = (s32[256]{0:T(256)S(1)}, s32[256]{0:T(256)}, u32[]{:S(2)}) copy-start(s32[256]{0:T(256)} %param.13) | copy-start | bytes 3076
  0.7 0.8 %copy-start = (f32[3,4096]{1,0:T(4,128)S(1)}, f32[3,4096]{1,0:T(4,128)}, u32[]{:S(2)}) copy-start(f32[3,4096]{1,0:T(4,128)} %pos_ref.1) | copy-start | bytes 147460
  1.5 0.8 %copy-start.1 = (f32[3,4096]{1,0:T(4,128)S(1)}, f32[3,4096]{1,0:T(4,128)}, u32[]{:S(2)}) copy-start(f32[3,4096]{1,0:T(4,128)} %vel_ref.1) | copy-start | bytes 147460
  2.4 0.8 %copy-start.2 = (f32[3,4096]{1,0:T(4,128)S(1)}, f32[3,4096]{1,0:T(4,128)}, u32[]{:S(2)}) copy-start(f32[3,4096]{1,0:T(4,128)} %acc_ref.1) | copy-start | bytes 147460
  3.2 0.8 %copy-start.3 = (f32[3,4096]{1,0:T(4,128)S(1)}, f32[3,4096]{1,0:T(4,128)}, u32[]{:S(2)}) copy-start(f32[3,4096]{1,0:T(4,128)} %jerk_ref.1) | copy-start | bytes 147460
  4.0 0.7 %copy-start.4 = (f32[4096]{0:T(1024)S(1)}, f32[4096]{0:T(1024)}, u32[]{:S(2)}) copy-start(f32[4096]{0:T(1024)} %param.11) | copy-start | bytes 49156
  4.8 0.7 %copy-start.5 = (f32[4096]{0:T(1024)S(1)}, f32[4096]{0:T(1024)}, u32[]{:S(2)}) copy-start(f32[4096]{0:T(1024)} %param.12) | copy-start | bytes 49156

commit v2 on v1

--- a/solution.py
+++ b/solution.py
@@ -84,14 +84,21 @@
 
 
 def kernel(
-    n_row, n_col, share, pos_ref, vel_ref, acc_ref, jerk_ref, mass_ref, step_ref, act_ref, out_ref,
-    idx, table, left, weight, mid_ref, give, got, state, f_give, f_got,
-    idx_s, idx_r, give_s, give_r, st_s, st_r, f_s, f_r,
+    n_row, n_col, share, *refs
 ):
+    far, out_ref, near, rest = refs[:7], refs[7], refs[8:15], refs[15:]
+    pos_ref, vel_ref, acc_ref, jerk_ref, mass_ref, step_ref, act_ref = near
+    (idx, table, left, weight, mid_ref, give, got, row_sum, col_got, own, state, f_give, f_got,
+     in_s, idx_s, idx_r, give_s, give_r, col_s, col_r, st_s, st_r, f_s, f_r) = rest
+    loads = [pltpu.make_async_copy(a, b, in_s.at[t]) for t, (a, b) in enumerate(zip(far, near))]
+    for load in loads:
+        load.start()
+
     n_dev = n_row * n_col
     bodies = pos_ref.shape[1]
     chunks = bodies // WIDE
     act_row = share * n_col
+    depth = min(256, bodies)
     row, col = lax.axis_index("row"), lax.axis_index("col")
     me = row * n_col + col
     base = me * bodies
@@ -114,6 +121,8 @@
         return 0
 
     lax.fori_loop(1, n_dev, greet, 0)
+    for load in loads:
+        load.wait()
 
     for c in range(chunks):
         lane = pl.ds(c * WIDE, WIDE)
@@ -136,8 +145,8 @@
     lax.fori_loop(1, n_row, idx_start, 0)
     idx[row] = act_ref[...]
 
-    def give_copy(d, slot):
-        return send(give.at[d], got.at[slot], give_s.at[d], give_r.at[slot], at(d))
+    def give_copy(r, slot):
+        return send(give.at[r], got.at[slot], give_s.at[r], give_r.at[slot], (r, col))
 
     def pick(k, _):
         r = lax.rem(row + k, n_row)
@@ -156,16 +165,11 @@
         mine = jnp.zeros((16, act_row), f32)
         for c in range(chunks):
             mine = mine + jnp.where(high == c, found[c * 16 : (c + 1) * 16], 0.0)
-        for c in range(n_col):
-            part = mine[:, c * share : (c + 1) * share]
-            d = r * n_col + c
-            give[d] = padded(jnp.concatenate([part[0:8], part[8:16]], axis=1), 8, WIDE)
-        for c in range(n_col):
-            d = r * n_col + c
-
-            @pl.when(d != me)
-            def _():
-                give_copy(d, me).start()
+        give[r] = mine
+
+        @pl.when(k > 0)
+        def _():
+            give_copy(r, row).start()
 
         return 0
 
@@ -185,55 +189,92 @@
         weight[:, lane] = weight_rows(p, q, mass_ref[:, lane]).astype(bf16)
 
     def gather(k, total):
-        d = other(k)
-        give_copy(d, d).wait_recv()
-        return total + got[d]
-
-    slab = lax.fori_loop(1, n_dev, gather, give[me])
-    x0, v0, a0 = slab[0:3, 0:share], slab[3:6, 0:share], jnp.concatenate(
-        [slab[6:8, 0:share], slab[0:1, share : 2 * share]], axis=0)
-    j0, step = slab[1:4, share : 2 * share], slab[4:5, share : 2 * share]
-    p_own, q_own = predict(x0, v0, a0, j0, step)
-    state[me] = padded(jnp.concatenate([p_own, q_own], axis=1), 4, WIDE)
-
-    def state_copy(d, slot):
-        return send(state.at[me], state.at[slot], st_s.at[d], st_r.at[slot], at(d))
+        r = lax.rem(row + k, n_row)
+        give_copy(r, r).wait_recv()
+        return total + got[r]
+
+    row_sum[...] = lax.fori_loop(1, n_row, gather, give[row])
+
+    def col_copy(c, slot):
+        return send(row_sum, col_got.at[slot], col_s.at[c], col_r.at[slot], (row, c))
+
+    for k in range(1, n_col):
+        col_copy(lax.rem(col + k, n_col), col).start()
+    col_got[col] = row_sum[...]
+    for k in range(1, n_col):
+        c = lax.rem(col + k, n_col)
+        col_copy(c, c).wait_recv()
+    slab = col_got[0]
+    for c in range(1, n_col):
+        slab = slab + col_got[c]
+    p_row, q_row = predict(slab[0:3], slab[3:6], slab[6:9], slab[9:12], slab[12:13])
+    state[row] = padded(jnp.concatenate([p_row, q_row], axis=0), 8, act_row)
+    for c in range(n_col):
+        own[c] = padded(slab[:, c * share : (c + 1) * share], 16, WIDE)
+
+    def state_copy(r, slot):
+        return send(state.at[row], state.at[slot], st_s.at[r], st_r.at[slot], (r, col))
 
     def state_start(k, _):
-        state_copy(other(k), me).start()
-        return 0
-
-    lax.fori_loop(1, n_dev, state_start, 0)
+        state_copy(lax.rem(row + k, n_row), row).start()
+        return 0
+
+    lax.fori_loop(1, n_row, state_start, 0)
+
+    def turn(k):
+        if n_row & (n_row - 1):
+            return lax.rem(row + k, n_row)
+        step_to = jnp.where(k == 0, 0, jnp.where(k == n_row - 1, 1, k + 1))
+        return lax.bitwise_xor(row, step_to)
 
     def f_copy(d, slot):
         return send(f_give.at[d], f_got.at[slot], f_s.at[d], f_r.at[slot], at(d))
 
     def meet(k, _):
-        r = lax.rem(row + k, n_row)
-        for c in range(n_col):
-            d = r * n_col + c
-
-            @pl.when(d != me)
-            def _():
-                state_copy(d, d).wait_recv()
-
-        slabs = [state[r * n_col + c] for c in range(n_col)]
-        p = jnp.concatenate([s[0:3, 0:share] for s in slabs], axis=1) - mid_ref[0:3, 0:1]
-        q = jnp.concatenate([s[0:3, share : 2 * share] for s in slabs], axis=1) - mid_ref[3:6, 0:1]
+        r = turn(k)
+
+        @pl.when(k > 0)
+        def _():
+            state_copy(r, r).wait_recv()
+
+        slab = state[r]
+        p = slab[0:3] - mid_ref[0:3, 0:1]
+        q = slab[3:6] - mid_ref[3:6, 0:1]
         for_sq, for_rw = active_rows(p, q)
-        b = left[...]
-        qt = weight[...]
-        dist_sq = jnp.dot(b, for_sq, preferred_element_type=f32)
-        r_dot_w = jnp.dot(b, for_rw, preferred_element_type=f32)
-        inv = lax.rsqrt(dist_sq)
-        inv_sq = inv * inv
-        w = inv_sq * inv
-        v = (w * inv_sq) * r_dot_w
-        wh, vh = w.astype(bf16), v.astype(bf16)
-        wl = (w - wh.astype(f32)).astype(bf16)
-        vl = (v - vh.astype(f32)).astype(bf16)
-        ws = jnp.dot(qt, wh, preferred_element_type=f32) + jnp.dot(qt, wl, preferred_element_type=f32)
-        vs = jnp.dot(qt, vh, preferred_element_type=f32) + jnp.dot(qt, vl, preferred_element_type=f32)
+
+        def products(t):
+            b = left[pl.ds(t * depth, depth), :]
+            return (
+                jnp.dot(b, for_sq, preferred_element_type=f32),
+                jnp.dot(b, for_rw, preferred_element_type=f32),
+            )
+
+        def kernels(dist_sq, r_dot_w):
+            inv = lax.rsqrt(dist_sq)
+            inv_sq = inv * inv
+            w = inv_sq * inv
+            v = (w * inv_sq) * r_dot_w
+            wh, vh = w.astype(bf16), v.astype(bf16)
+            wl = (w - wh.astype(f32)).astype(bf16)
+            vl = (v - vh.astype(f32)).astype(bf16)
+            return wh, wl, vh, vl
+
+        def sums(total, t, parts):
+            qt = weight[:, pl.ds(t * depth, depth)]
+            wh, wl, vh, vl = [jnp.dot(qt, x, preferred_element_type=f32) for x in parts]
+            return total[0] + (wh + wl), total[1] + (vh + vl)
+
+        blocks = bodies // depth
+        zero = jnp.zeros((32, act_row), f32)
+        total = (zero, zero)
+        now, held = products(0), None
+        for t in range(blocks):
+            later = products(t + 1) if t + 1 < blocks else None
+            parts = kernels(*now)
+            if held is not None:
+                total = sums(total, t - 1, held)
+            now, held = later, parts
+        ws, vs = sums(total, blocks - 1, held)
         w_sum = ws[18:19] + ws[19:20] + ws[20:21]
         v_sum = vs[18:19] + vs[19:20] + vs[20:21]
         acc = three(ws, 0) - p * w_sum
@@ -259,21 +300,25 @@
 
     forces = lax.fori_loop(1, n_dev, add_up, f_give[me])
     a1, j1 = forces[0:3, 0:share], forces[0:3, share : 2 * share]
+    body = own[col][:, 0:share]
+    x0, v0, a0, j0, step = body[0:3], body[3:6], body[6:9], body[9:12], body[12:13]
     v1 = v0 + step / 2.0 * (a0 + a1) + step * step / 12.0 * (j0 - j1)
     x1 = x0 + step / 2.0 * (v0 + v1) + step * step / 12.0 * (a0 - a1)
     out_ref[...] = jnp.concatenate([x1, v1, a1, j1], axis=0)
 
-    def idx_end(k, _):
-        idx_copy(lax.rem(row + k, n_row), row).wait_send()
-        return 0
-
-    lax.fori_loop(1, n_row, idx_end, 0)
+    def row_end(k, _):
+        r = lax.rem(row + k, n_row)
+        idx_copy(r, row).wait_send()
+        give_copy(r, row).wait_send()
+        state_copy(r, row).wait_send()
+        return 0
+
+    lax.fori_loop(1, n_row, row_end, 0)
+    for k in range(1, n_col):
+        col_copy(lax.rem(col + k, n_col), col).wait_send()
 
     def all_end(k, _):
-        d = other(k)
-        give_copy(d, me).wait_send()
-        state_copy(d, me).wait_send()
-        f_copy(d, me).wait_send()
+        f_copy(other(k), me).wait_send()
         return 0
 
     lax.fori_loop(1, n_dev, all_end, 0)
@@ -291,26 +336,38 @@
         return pl.pallas_call(
             functools.partial(kernel, n_row, n_col, share),
             out_shape=jax.ShapeDtypeStruct((12, share), f32),
-            in_specs=[pl.BlockSpec(memory_space=pltpu.VMEM)] * 7,
+            in_specs=[pl.BlockSpec(memory_space=pltpu.MemorySpace.HBM)] * 7,
             out_specs=pl.BlockSpec(memory_space=pltpu.VMEM),
             scratch_shapes=[
+                pltpu.VMEM((3, bodies), f32),
+                pltpu.VMEM((3, bodies), f32),
+                pltpu.VMEM((3, bodies), f32),
+                pltpu.VMEM((3, bodies), f32),
+                pltpu.VMEM((1, bodies), f32),
+                pltpu.VMEM((1, bodies), f32),
+                pltpu.VMEM((1, act_row), jnp.int32),
                 pltpu.VMEM((n_row, 1, act_row), jnp.int32),
                 pltpu.VMEM((3, bodies // WIDE * 16, WIDE), bf16),
                 pltpu.VMEM((bodies, WIDE), bf16),
                 pltpu.VMEM((32, bodies), bf16),
                 pltpu.VMEM((8, WIDE), f32),
-                pltpu.VMEM((n_dev, 8, WIDE), f32),
-                pltpu.VMEM((n_dev, 8, WIDE), f32),
+                pltpu.VMEM((n_row, 16, act_row), f32),
+                pltpu.VMEM((n_row, 16, act_row), f32),
+                pltpu.VMEM((16, act_row), f32),
+                pltpu.VMEM((n_col, 16, act_row), f32),
+                pltpu.VMEM((n_col, 16, WIDE), f32),
+                pltpu.VMEM((n_row, 8, act_row), f32),
                 pltpu.VMEM((n_dev, 4, WIDE), f32),
                 pltpu.VMEM((n_dev, 4, WIDE), f32),
-                pltpu.VMEM((n_dev, 4, WIDE), f32),
+                dma((7,)),
                 dma((n_row,)), dma((n_row,)),
-                dma((n_dev,)), dma((n_dev,)),
-                dma((n_dev,)), dma((n_dev,)),
+                dma((n_row,)), dma((n_row,)),
+                dma((n_col,)), dma((n_col,)),
+                dma((n_row,)), dma((n_row,)),
                 dma((n_dev,)), dma((n_dev,)),
             ],
             compiler_params=pltpu.CompilerParams(
-                collective_id=0, has_side_effects=True, vmem_limit_bytes=48 * 2**20
+                collective_id=0, has_side_effects=True, vmem_limit_bytes=67043328
             ),
         )(position, velocity, accel, jerk, mass[None, :], elapsed[None, :], active[None, :])
 

time: 54.6 us -> 45.9 us (0.84)
  local copies, waits for them, and re-layouts: 6.07 us -> 1.3 us
  Pallas kernels: 48.1 us -> 44.4 us
    unnamed x15 -> x1, local copies, waits for them, and re-layouts: 6.07 us -> 1.3 us
    pallas_call x1, Pallas kernels: 48.1 us -> 44.4 us  [local(): pl.pallas_call(functools.partial(kernel, n_row, n_col, share), out_shape=...]
where the time goes in v2:
time: 45.9 us; the launch traced here: 45.7 us
  Pallas kernels  44.4 us (97%)
  local copies, waits for them, and re-layouts  1.3 us (3%)
    pallas_call x1, Pallas kernels, local(): pl.pallas_call(functools.partial(kernel, n_row, n_col, share), out_shape=...  44.4 us
    unnamed x1, local copies, waits for them, and re-layouts  1.3 us

profile of v2, /device:TPU:1, one launch (start us, length us, event | category | flops | bytes accessed | tf_op | source)
XLA Modules:
  0.0 45.7 jit_solution(284024309671292452)
XLA Ops:
  0.0 44.4 %shard_map.73 = f32[12,64]{1,0:T(8,128)} custom-call(f32[3,4096]{1,0:T(4,128)} %refs_0_.1, f32[3,4096]{1,0:T(4,128)} %refs_1_.1, f32[3,4096]{1,0:T(4,128)} %refs_2_.1, f32[3,4096]{1,0:T(4,128)} %refs_3_.1, f32[1,4096]{1,0:T(1,128)} %bitcast.3, f32[1,4096]{1,0:T(1,128)} %bitcast.4, s32[1,256]{1,0:T(1,128)} %bitcast.5), custom_call_target="tpu_custom_call" | custom-call | tf_op jit(solution)/shard_map/pallas_call | solution.py:336
  44.4 1.3 %copy.9 = f32[12,64]{1,0:T(8,128)} copy(f32[12,64]{1,0:T(8,128)} %shard_map.73) | data formatting | bytes 6144

commit v3 on v2

--- a/solution.py
+++ b/solution.py
@@ -88,8 +88,8 @@
 ):
     far, out_ref, near, rest = refs[:7], refs[7], refs[8:15], refs[15:]
     pos_ref, vel_ref, acc_ref, jerk_ref, mass_ref, step_ref, act_ref = near
-    (idx, table, left, weight, mid_ref, give, got, row_sum, col_got, own, state, f_give, f_got,
-     in_s, idx_s, idx_r, give_s, give_r, col_s, col_r, st_s, st_r, f_s, f_r) = rest
+    (idx, table, left, weight, mid_ref, give, got, row_sum, col_got, own, own_got, state, f_give, f_got,
+     in_s, idx_s, idx_r, give_s, give_r, col_s, col_r, own_s, own_r, st_s, st_r, f_s, f_r) = rest
     loads = [pltpu.make_async_copy(a, b, in_s.at[t]) for t, (a, b) in enumerate(zip(far, near))]
     for load in loads:
         load.start()
@@ -117,10 +117,12 @@
     barrier = pltpu.get_barrier_semaphore()
 
     def greet(k, _):
-        pl.semaphore_signal(barrier, inc=1, device_id=at(other(k)), device_id_type=MESH)
-        return 0
-
-    lax.fori_loop(1, n_dev, greet, 0)
+        pl.semaphore_signal(barrier, inc=1, device_id=(lax.rem(row + k, n_row), col), device_id_type=MESH)
+        return 0
+
+    lax.fori_loop(1, n_row, greet, 0)
+    for k in range(1, n_col):
+        pl.semaphore_signal(barrier, inc=1, device_id=(row, lax.rem(col + k, n_col)), device_id_type=MESH)
     for load in loads:
         load.wait()
 
@@ -131,9 +133,9 @@
              jnp.zeros((3, WIDE), f32)], axis=0,
         )
         for t, piece in enumerate(split3(raw)):
-            table[t, pl.ds(c * 16, 16), :] = piece.astype(bf16)
-
-    pl.semaphore_wait(barrier, n_dev - 1)
+            table[pl.ds(c * 16, 16), pl.ds(t * WIDE, WIDE)] = piece.astype(bf16)
+
+    pl.semaphore_wait(barrier, n_row - 1 + n_col - 1)
 
     def idx_copy(r, slot):
         return send(act_ref, idx.at[slot], idx_s.at[r], idx_r.at[slot], (r, col))
@@ -159,9 +161,7 @@
         high = lax.shift_right_arithmetic(offset, 7)
         low = lax.bitwise_and(offset, 127)
         hot = jnp.where(lax.broadcasted_iota(jnp.int32, (WIDE, act_row), 0) == low, 1.0, 0.0).astype(bf16)
-        found = jnp.dot(table[0], hot, preferred_element_type=f32)
-        found = found + jnp.dot(table[1], hot, preferred_element_type=f32)
-        found = found + jnp.dot(table[2], hot, preferred_element_type=f32)
+        found = jnp.dot(table[...], jnp.concatenate([hot, hot, hot], axis=0), preferred_element_type=f32)
         mine = jnp.zeros((16, act_row), f32)
         for c in range(chunks):
             mine = mine + jnp.where(high == c, found[c * 16 : (c + 1) * 16], 0.0)
@@ -193,24 +193,28 @@
         give_copy(r, r).wait_recv()
         return total + got[r]
 
-    row_sum[...] = lax.fori_loop(1, n_row, gather, give[row])
+    slab = lax.fori_loop(1, n_row, gather, give[row])
+    p_row, q_row = predict(slab[0:3], slab[3:6], slab[6:9], slab[9:12], slab[12:13])
+    row_sum[...] = padded(jnp.concatenate([p_row, q_row], axis=0), 8, act_row)
 
     def col_copy(c, slot):
         return send(row_sum, col_got.at[slot], col_s.at[c], col_r.at[slot], (row, c))
 
+    def own_copy(c, slot):
+        return send(own.at[c], own_got.at[slot], own_s.at[c], own_r.at[slot], (row, c))
+
     for k in range(1, n_col):
         col_copy(lax.rem(col + k, n_col), col).start()
+    for c in range(n_col):
+        own[c] = padded(slab[:, c * share : (c + 1) * share], 16, WIDE)
     col_got[col] = row_sum[...]
     for k in range(1, n_col):
         c = lax.rem(col + k, n_col)
         col_copy(c, c).wait_recv()
-    slab = col_got[0]
+    total_state = col_got[0]
     for c in range(1, n_col):
-        slab = slab + col_got[c]
-    p_row, q_row = predict(slab[0:3], slab[3:6], slab[6:9], slab[9:12], slab[12:13])
-    state[row] = padded(jnp.concatenate([p_row, q_row], axis=0), 8, act_row)
-    for c in range(n_col):
-        own[c] = padded(slab[:, c * share : (c + 1) * share], 16, WIDE)
+        total_state = total_state + col_got[c]
+    state[row] = total_state
 
     def state_copy(r, slot):
         return send(state.at[row], state.at[slot], st_s.at[r], st_r.at[slot], (r, col))
@@ -220,6 +224,8 @@
         return 0
 
     lax.fori_loop(1, n_row, state_start, 0)
+    for k in range(1, n_col):
+        own_copy(lax.rem(col + k, n_col), col).start()
 
     def turn(k):
         if n_row & (n_row - 1):
@@ -300,7 +306,12 @@
 
     forces = lax.fori_loop(1, n_dev, add_up, f_give[me])
     a1, j1 = forces[0:3, 0:share], forces[0:3, share : 2 * share]
-    body = own[col][:, 0:share]
+    body = own[col]
+    for k in range(1, n_col):
+        c = lax.rem(col + k, n_col)
+        own_copy(c, c).wait_recv()
+        body = body + own_got[c]
+    body = body[:, 0:share]
     x0, v0, a0, j0, step = body[0:3], body[3:6], body[6:9], body[9:12], body[12:13]
     v1 = v0 + step / 2.0 * (a0 + a1) + step * step / 12.0 * (j0 - j1)
     x1 = x0 + step / 2.0 * (v0 + v1) + step * step / 12.0 * (a0 - a1)
@@ -315,7 +326,9 @@
 
     lax.fori_loop(1, n_row, row_end, 0)
     for k in range(1, n_col):
-        col_copy(lax.rem(col + k, n_col), col).wait_send()
+        c = lax.rem(col + k, n_col)
+        col_copy(c, col).wait_send()
+        own_copy(c, col).wait_send()
 
     def all_end(k, _):
         f_copy(other(k), me).wait_send()
@@ -347,14 +360,15 @@
                 pltpu.VMEM((1, bodies), f32),
                 pltpu.VMEM((1, act_row), jnp.int32),
                 pltpu.VMEM((n_row, 1, act_row), jnp.int32),
-                pltpu.VMEM((3, bodies // WIDE * 16, WIDE), bf16),
+                pltpu.VMEM((bodies // WIDE * 16, 3 * WIDE), bf16),
                 pltpu.VMEM((bodies, WIDE), bf16),
                 pltpu.VMEM((32, bodies), bf16),
                 pltpu.VMEM((8, WIDE), f32),
                 pltpu.VMEM((n_row, 16, act_row), f32),
                 pltpu.VMEM((n_row, 16, act_row), f32),
-                pltpu.VMEM((16, act_row), f32),
-                pltpu.VMEM((n_col, 16, act_row), f32),
+                pltpu.VMEM((8, act_row), f32),
+                pltpu.VMEM((n_col, 8, act_row), f32),
+                pltpu.VMEM((n_col, 16, WIDE), f32),
                 pltpu.VMEM((n_col, 16, WIDE), f32),
                 pltpu.VMEM((n_row, 8, act_row), f32),
                 pltpu.VMEM((n_dev, 4, WIDE), f32),
@@ -363,6 +377,7 @@
                 dma((n_row,)), dma((n_row,)),
                 dma((n_row,)), dma((n_row,)),
                 dma((n_col,)), dma((n_col,)),
+                dma((n_col,)), dma((n_col,)),
                 dma((n_row,)), dma((n_row,)),
                 dma((n_dev,)), dma((n_dev,)),
             ],

time: 45.9 us -> 44.9 us (0.978)
  Pallas kernels: 44.4 us -> 43.3 us
    pallas_call x1, Pallas kernels: 44.4 us -> 43.3 us  [local(): pl.pallas_call(functools.partial(kernel, n_row, n_col, share), out_shape=...]
where the time goes in v3:
time: 44.9 us; the launch traced here: 44.7 us
  Pallas kernels  43.3 us (96%)
  local copies, waits for them, and re-layouts  1.3 us (3%)
    pallas_call x1, Pallas kernels, local(): pl.pallas_call(functools.partial(kernel, n_row, n_col, share), out_shape=...  43.3 us
    unnamed x1, local copies, waits for them, and re-layouts  1.3 us

profile of v3, /device:TPU:1, one launch (start us, length us, event | category | flops | bytes accessed | tf_op | source)
XLA Modules:
  0.0 44.7 jit_solution(499848181789499743)
XLA Ops:
  0.0 43.3 %shard_map.73 = f32[12,64]{1,0:T(8,128)} custom-call(f32[3,4096]{1,0:T(4,128)} %refs_0_.1, f32[3,4096]{1,0:T(4,128)} %refs_1_.1, f32[3,4096]{1,0:T(4,128)} %refs_2_.1, f32[3,4096]{1,0:T(4,128)} %refs_3_.1, f32[1,4096]{1,0:T(1,128)} %bitcast.3, f32[1,4096]{1,0:T(1,128)} %bitcast.4, s32[1,256]{1,0:T(1,128)} %bitcast.5), custom_call_target="tpu_custom_call" | custom-call | tf_op jit(solution)/shard_map/pallas_call | solution.py:349
  43.4 1.3 %copy.9 = f32[12,64]{1,0:T(8,128)} copy(f32[12,64]{1,0:T(8,128)} %shard_map.73) | data formatting | bytes 6144
